TPU v7x, 256 devices: a whole 4x4x8 slice. The times are simulated.
256 devices in a mesh: dom: 16 (over y, z_lo, core), dir: 16 (over x, z_hi).
Axes of the slice: x: 4, y: 4, z: 8 (z_hi: 4, z_lo: 2; z = z_hi * 2 + z_lo), core: 2. Of those that a mesh axis runs over, the one named last changes fastest.
Arguments:
- coefficients: bfloat16 [2, 70, 32768], P(None, None, ('dom', 'dir')), may hold values from -6 to 6
- positions: float32 [3, 32768], P(None, ('dom', 'dir')), may hold values from -50 to 50
- polar: float32 [10240], P('dir'), may hold values from 0 to 1.4
- azimuth: float32 [10240], P('dir'), may hold values from -3.140625 to 3.140625
- weights: float32 [10240], P('dir'), may hold values from -4 to 4
- farmap: float32 [2, 2, 70, 10240], P(None, None, None, 'dir'), may hold values from -0.00390625 to 0.00390625
Outputs:
- coef_grad: float32 [2, 70, 32768], P(None, None, ('dom', 'dir'))
- place_grad: float32 [3, 32768], P(None, ('dom', 'dir'))
All inputs are finite; a program needn't handle non-finite values.
Results may differ from a plain program's by a relative error of at most 0.0052.
Values may be sent and summed in bfloat16 or wider, within the bound.
A program may use at most 64 MiB of HBM per device.

v0:
```python
import jax
import jax.numpy as jnp
from jax import lax
from jax.sharding import PartitionSpec as P

C = 70


def unit_vectors(polar, azimuth):
    sine_polar = jnp.sin(polar)
    return jnp.stack([sine_polar * jnp.cos(azimuth), sine_polar * jnp.sin(azimuth), jnp.cos(polar)])


def phase_tile(places, vectors):
    angles = (
        places[0][:, None] * vectors[0][None, :]
        + places[1][:, None] * vectors[1][None, :]
        + places[2][:, None] * vectors[2][None, :]
    )
    return (jnp.cos(angles).astype(jnp.bfloat16), jnp.sin(angles).astype(jnp.bfloat16))


def field_terms(coef_block, cos_tile, sin_tile):
    order_count = coef_block.shape[0] // 2
    real_rows = coef_block[:order_count]
    imag_rows = coef_block[order_count:]
    top_rows = jnp.concatenate([real_rows, imag_rows], axis=1)
    low_rows = jnp.concatenate([imag_rows, -real_rows], axis=1)
    left_side = jnp.concatenate([top_rows, low_rows], axis=0)
    right_side = jnp.concatenate([cos_tile, sin_tile], axis=0)
    return jnp.dot(left_side, right_side, preferred_element_type=jnp.float32)


def adjoint_terms(stacked, cos_tile, sin_tile):
    order_count = stacked.shape[0] // 2
    real_rows = stacked[:order_count]
    imag_rows = stacked[order_count:]
    top_rows = jnp.concatenate([real_rows, imag_rows], axis=1)
    low_rows = jnp.concatenate([imag_rows, -real_rows], axis=1)
    left_side = jnp.concatenate([top_rows, low_rows], axis=0)
    right_side = jnp.concatenate([cos_tile, sin_tile], axis=1)
    return lax.dot_general(
        left_side, right_side, (((1,), (1,)), ((), ())), preferred_element_type=jnp.float32
    )


def amplitude_parts(fields, farmap):
    order_count = fields.shape[0] // 2
    field_real = fields[:order_count][None]
    field_imag = fields[order_count:][None]
    map_real = farmap[:, 0]
    map_imag = farmap[:, 1]
    amp_real = jnp.sum(map_real * field_real - map_imag * field_imag, axis=1)
    amp_imag = jnp.sum(map_real * field_imag + map_imag * field_real, axis=1)
    return (amp_real, amp_imag)


def cotangent_from(amp_real, amp_imag, farmap, weights):
    map_real = farmap[:, 0]
    map_imag = farmap[:, 1]
    cot_real = weights * jnp.sum(
        amp_real[:, None] * map_real + amp_imag[:, None] * map_imag, axis=0
    )
    cot_imag = weights * jnp.sum(
        amp_real[:, None] * map_imag - amp_imag[:, None] * map_real, axis=0
    )
    return jnp.concatenate([cot_real, cot_imag], axis=0).astype(jnp.bfloat16)


def cotangent_rows(fields, farmap, weights):
    amp_real, amp_imag = amplitude_parts(fields, farmap)
    return cotangent_from(amp_real, amp_imag, farmap, weights)


def stacked_rows(adjoint, vectors):
    order_count = adjoint.shape[0] // 2
    widened = adjoint.astype(jnp.float32)
    scaled = [(vectors[axis_id][None, :] * widened).astype(jnp.bfloat16) for axis_id in range(3)]
    real_parts = [adjoint[:order_count]] + [item[:order_count] for item in scaled]
    imag_parts = [adjoint[order_count:]] + [item[order_count:] for item in scaled]
    return jnp.concatenate(real_parts + imag_parts, axis=0)


def gradients(output, coef_block):
    order_count = coef_block.shape[0] // 2
    real_out = output[: 4 * order_count]
    imag_out = output[4 * order_count :]
    coef_term = jnp.concatenate(
        [2.0 * real_out[:order_count], -2.0 * imag_out[:order_count]], axis=0
    )
    coef_real = coef_block[:order_count].astype(jnp.float32)
    coef_imag = coef_block[order_count:].astype(jnp.float32)
    place_terms = []
    for axis_id in range(3):
        lower_row = (axis_id + 1) * order_count
        upper_row = (axis_id + 2) * order_count
        place_terms.append(
            2.0
            * jnp.sum(
                coef_real * imag_out[lower_row:upper_row]
                + coef_imag * real_out[lower_row:upper_row],
                axis=0,
            )
        )
    return (coef_term, jnp.stack(place_terms))


def body(coefficients, positions, polar, azimuth, weights, farmap):
    own_count = coefficients.shape[2]
    own_rows = coefficients.reshape(2 * C, own_count)
    domain_rows = lax.all_gather(own_rows, "dir", axis=1, tiled=True)
    domain_places = lax.all_gather(positions, "dir", axis=1, tiled=True)
    vectors = unit_vectors(polar, azimuth)
    width_all = domain_rows.shape[1]
    width_block = 512
    blocks = width_all // width_block

    def forward_block(block_id, totals):
        offset = block_id * width_block
        coef_block = lax.dynamic_slice_in_dim(domain_rows, offset, width_block, 1)
        place_block = lax.dynamic_slice_in_dim(domain_places, offset, width_block, 1)
        cos_tile, sin_tile = phase_tile(place_block, vectors)
        return totals + field_terms(coef_block, cos_tile, sin_tile)

    partial_fields = lax.fori_loop(
        0, blocks, forward_block, jnp.zeros((2 * C, polar.shape[0]), jnp.float32)
    )
    fields = lax.psum(partial_fields, "dom")
    adjoint = cotangent_rows(fields, farmap, weights)
    stacked = stacked_rows(adjoint, vectors)

    def backward_block(block_id):
        offset = block_id * width_block
        coef_block = lax.dynamic_slice_in_dim(domain_rows, offset, width_block, 1)
        place_block = lax.dynamic_slice_in_dim(domain_places, offset, width_block, 1)
        cos_tile, sin_tile = phase_tile(place_block, vectors)
        return gradients(adjoint_terms(stacked, cos_tile, sin_tile), coef_block)

    coef_parts, place_parts = lax.map(backward_block, jnp.arange(blocks, dtype=jnp.int32))
    coef_part = jnp.moveaxis(coef_parts, 0, 1).reshape(2 * C, width_all)
    place_part = jnp.moveaxis(place_parts, 0, 1).reshape(3, width_all)
    coef_grad, place_grad = (
        lax.psum_scatter(coef_part, "dir", scatter_dimension=1, tiled=True),
        lax.psum_scatter(place_part, "dir", scatter_dimension=1, tiled=True),
    )
    return (coef_grad.reshape(2, C, own_count), place_grad)


def solution(mesh):
    placed = (
        P(None, None, ("dom", "dir")),
        P(None, ("dom", "dir")),
        P("dir"),
        P("dir"),
        P("dir"),
        P(None, None, None, "dir"),
    )
    return jax.shard_map(
        body,
        mesh=mesh,
        in_specs=placed,
        out_specs=(P(None, None, ("dom", "dir")), P(None, ("dom", "dir"))),
        check_vma=False,
    )
```

profile of v0, /device:TPU:8, one launch (start us, length us, event | category | flops | bytes accessed | tf_op | source)
XLA Modules:
  0.0 478.9 jit_solution(2724014570653692775)
XLA Ops:
  7.2 0.7 fusion.36
  7.9 0.7 sine_multiply_fusion
  8.7 0.8 copy.18
  9.5 50.1 %all_gather.7 = bf16[140,2048]{1,0:T(8,128)(2,1)S(1)} all-gather(bf16[140,128]{1,0:T(8,128)(2,1)S(1)} %reshape.65), channel_id=1, replica_groups=mesh['dom'=16,'dir'=16] {'dir'}, dimensions={1}, use_global_device_ids=true | all-gather | bytes 609280 | tf_op jit(solution)/shard_map/all_gather | solution.py:111
  59.6 38.4 %all_gather.6 = f32[3,2048]{1,0:T(4,128)S(1)} all-gather(f32[3,128]{1,0:T(4,128)} %param.11), channel_id=1, replica_groups=mesh['dom'=16,'dir'=16] {'dir'}, dimensions={1}, use_global_device_ids=true | all-gather | bytes 26112 | tf_op jit(solution)/shard_map/all_gather | solution.py:112
  98.0 24.7 %while.29 = (s32[]{:T(128)}, f32[140,640]{1,0:T(8,128)S(1)}, bf16[140,2048]{1,0:T(8,128)(2,1)S(1)}, f32[3,2048]{1,0:T(4,128)S(1)}, f32[1,640]{1,0:T(1,128)S(1)},...) while((s32[]{:T(128)}, f32[140,640]{1,0:T(8,128)S(1)}, ...), condition=%wide.region_1.0_spmd.clone, body=%wide.region_0.0_spmd.clone.sunk | while | flops 189849616 | bytes 3953417 | solution.py:125
  98.2 5.4 %cosine_convert_fusion.5 = (bf16[512,640]{1,0:T(8,128)(2,1)S(1)}, bf16[512,640]{1,0:T(8,128)(2,1)S(1)}) fusion(f32[640]{0:T(1024)S(1)} %reduce.15, f32[512]{0:T(512)S(1)} %bitcast.83, f32[640]{0:T(1024)S(1)} %reduce.16, f32[512]{0:T(512)S(1)} %bitcast.82, f32[640]{0:T(1024)S(1)} %reduce.17, f32[512]{0:T(512)S(1)} %bitcast.81), kind=kLoop, calls=%fused_computation.35.clone.1 | loop fusion | flops 2293760 | bytes 1324544 | tf_op jit(solution)/shard_map/while/body/eval_jaxpr/convert_element_type | solution.py:20
  103.7 0.4 fusion.55
  104.3 5.4 %cosine_convert_fusion.5 = (bf16[512,640]{1,0:T(8,128)(2,1)S(1)}, bf16[512,640]{1,0:T(8,128)(2,1)S(1)}) fusion(f32[640]{0:T(1024)S(1)} %reduce.15, f32[512]{0:T(512)S(1)} %bitcast.83, f32[640]{0:T(1024)S(1)} %reduce.16, f32[512]{0:T(512)S(1)} %bitcast.82, f32[640]{0:T(1024)S(1)} %reduce.17, f32[512]{0:T(512)S(1)} %bitcast.81), kind=kLoop, calls=%fused_computation.35.clone.1 | loop fusion | flops 2293760 | bytes 1324544 | tf_op jit(solution)/shard_map/while/body/eval_jaxpr/convert_element_type | solution.py:20
  109.9 0.4 fusion.55
  110.5 5.4 %cosine_convert_fusion.5 = (bf16[512,640]{1,0:T(8,128)(2,1)S(1)}, bf16[512,640]{1,0:T(8,128)(2,1)S(1)}) fusion(f32[640]{0:T(1024)S(1)} %reduce.15, f32[512]{0:T(512)S(1)} %bitcast.83, f32[640]{0:T(1024)S(1)} %reduce.16, f32[512]{0:T(512)S(1)} %bitcast.82, f32[640]{0:T(1024)S(1)} %reduce.17, f32[512]{0:T(512)S(1)} %bitcast.81), kind=kLoop, calls=%fused_computation.35.clone.1 | loop fusion | flops 2293760 | bytes 1324544 | tf_op jit(solution)/shard_map/while/body/eval_jaxpr/convert_element_type | solution.py:20
  116.1 0.4 fusion.55
  116.7 5.4 %cosine_convert_fusion.5 = (bf16[512,640]{1,0:T(8,128)(2,1)S(1)}, bf16[512,640]{1,0:T(8,128)(2,1)S(1)}) fusion(f32[640]{0:T(1024)S(1)} %reduce.15, f32[512]{0:T(512)S(1)} %bitcast.83, f32[640]{0:T(1024)S(1)} %reduce.16, f32[512]{0:T(512)S(1)} %bitcast.82, f32[640]{0:T(1024)S(1)} %reduce.17, f32[512]{0:T(512)S(1)} %bitcast.81), kind=kLoop, calls=%fused_computation.35.clone.1 | loop fusion | flops 2293760 | bytes 1324544 | tf_op jit(solution)/shard_map/while/body/eval_jaxpr/convert_element_type | solution.py:20
  122.2 0.4 fusion.55
  122.7 0.7 copy-done.1
  123.4 0.2 reduce-scatter.7.cloned.1.call-start
  123.7 0.6 fusion.31
  124.3 113.6 %all-reduce.2.cloned.1.call-done = f32[140,640]{1,0:T(8,128)} async-done(((f32[140,640]{1,0:T(8,128)}), f32[140,640]{1,0:T(8,128)}) %all-reduce.2.cloned.1.call-update) | async-done | bytes 358416 | tf_op jit(solution)/shard_map/psum | solution.py:128
  237.9 1.0 fusion.32
  239.5 14.7 %maximum_maximum_fusion = bf16[560,1280]{1,0:T(8,128)(2,1)S(1)} fusion(bf16[280,640]{1,0:T(8,128)(2,1)S(1)} %maximum_negate_fusion, bf16[70,640]{1,0:T(8,128)(2,1)S(1)} %get-tuple-element.343, bf16[70,640]{1,0:T(8,128)(2,1)S(1)} %get-tuple-element.355, bf16[70,640]{1,0:T(8,128)(2,1)S(1)} %get-tuple-element.339, bf16[70,640]{1,0:T(8,128)(2,1)S(1)} %get-tuple-element.351, ...), kind=kLoop, calls=%fused_computation.48 | loop fusion | flops 18636800 | bytes 2508800 | tf_op jit(solution)/shard_map/while/body/eval_jaxpr/concatenate | solution.py:40
  254.2 35.1 %while.28 = (s32[]{:T(128)}, f32[4,140,512]{2,1,0:T(8,128)}, f32[4,3,512]{2,1,0:T(4,128)S(1)}, s32[4]{0:T(128)S(1)}, f32[3,2048]{1,0:T(4,128)S(1)}, /*index=5*/f...) while((s32[]{:T(128)}, f32[4,140,512]{2,1,0:T(8,128)}, ...), condition=%wide.region_11.12_spmd, body=%wide.region_7.11_spmd.sunk | while | flops 739566592 | bytes 7435559 | solution.py:139
  254.2 0.6 dynamic_slice.33
  255.6 5.4 %cosine_convert_fusion.4 = (bf16[512,640]{1,0:T(8,128)(2,1)S(1)}, bf16[512,640]{1,0:T(8,128)(2,1)S(1)}) fusion(f32[640]{0:T(1024)S(1)} %reduce.12, f32[512]{0:T(512)S(1)} %bitcast.86, f32[640]{0:T(1024)S(1)} %reduce.13, f32[512]{0:T(512)S(1)} %bitcast.85, f32[640]{0:T(1024)S(1)} %reduce.14, f32[512]{0:T(512)S(1)} %bitcast.84), kind=kLoop, calls=%fused_computation.5.clone.1 | loop fusion | flops 2293760 | bytes 1324544 | tf_op jit(solution)/shard_map/while/body/eval_jaxpr/convert_element_type | solution.py:20
  261.1 0.9 convolution_bitcast_fusion.2
  262.0 0.2 fusion.49
  262.3 0.7 fusion.50
  263.0 0.6 dynamic_slice.33
  264.4 5.4 %cosine_convert_fusion.4 = (bf16[512,640]{1,0:T(8,128)(2,1)S(1)}, bf16[512,640]{1,0:T(8,128)(2,1)S(1)}) fusion(f32[640]{0:T(1024)S(1)} %reduce.12, f32[512]{0:T(512)S(1)} %bitcast.86, f32[640]{0:T(1024)S(1)} %reduce.13, f32[512]{0:T(512)S(1)} %bitcast.85, f32[640]{0:T(1024)S(1)} %reduce.14, f32[512]{0:T(512)S(1)} %bitcast.84), kind=kLoop, calls=%fused_computation.5.clone.1 | loop fusion | flops 2293760 | bytes 1324544 | tf_op jit(solution)/shard_map/while/body/eval_jaxpr/convert_element_type | solution.py:20
  269.9 0.9 convolution_bitcast_fusion.2
  270.8 0.2 fusion.49
  271.1 0.7 fusion.50
  271.8 0.6 dynamic_slice.33
  273.2 5.4 %cosine_convert_fusion.4 = (bf16[512,640]{1,0:T(8,128)(2,1)S(1)}, bf16[512,640]{1,0:T(8,128)(2,1)S(1)}) fusion(f32[640]{0:T(1024)S(1)} %reduce.12, f32[512]{0:T(512)S(1)} %bitcast.86, f32[640]{0:T(1024)S(1)} %reduce.13, f32[512]{0:T(512)S(1)} %bitcast.85, f32[640]{0:T(1024)S(1)} %reduce.14, f32[512]{0:T(512)S(1)} %bitcast.84), kind=kLoop, calls=%fused_computation.5.clone.1 | loop fusion | flops 2293760 | bytes 1324544 | tf_op jit(solution)/shard_map/while/body/eval_jaxpr/convert_element_type | solution.py:20
  278.6 0.9 convolution_bitcast_fusion.2
  279.6 0.2 fusion.49
  279.9 0.7 fusion.50
  280.6 0.6 dynamic_slice.33
  282.0 5.4 %cosine_convert_fusion.4 = (bf16[512,640]{1,0:T(8,128)(2,1)S(1)}, bf16[512,640]{1,0:T(8,128)(2,1)S(1)}) fusion(f32[640]{0:T(1024)S(1)} %reduce.12, f32[512]{0:T(512)S(1)} %bitcast.86, f32[640]{0:T(1024)S(1)} %reduce.13, f32[512]{0:T(512)S(1)} %bitcast.85, f32[640]{0:T(1024)S(1)} %reduce.14, f32[512]{0:T(512)S(1)} %bitcast.84), kind=kLoop, calls=%fused_computation.5.clone.1 | loop fusion | flops 2293760 | bytes 1324544 | tf_op jit(solution)/shard_map/while/body/eval_jaxpr/convert_element_type | solution.py:20
  287.4 0.9 convolution_bitcast_fusion.2
  288.6 0.7 fusion.50
  289.4 1.4 copy.23
  290.8 2.0 copy.20
  293.1 1.4 copy.27
  294.5 87.7 %reduce-scatter.7.cloned.1.call-done = f32[128,3]{1,0:T(8,128)} async-done(((f32[2048,3]{1,0:T(8,128)}), f32[128,3]{1,0:T(8,128)}) %reduce-scatter.7.cloned.1.call-update) | async-done | bytes 1552
  382.2 1.5 copy.24
  383.7 87.1 %reduce-scatter.5.cloned.1.call-done = f32[140,128]{1,0:T(8,128)} async-done(((f32[140,2048]{1,0:T(8,128)}), f32[140,128]{1,0:T(8,128)}) %reduce-scatter.5.cloned.1.call-update) | async-done | bytes 71696 | tf_op jit(solution)/shard_map/reduce_scatter | solution.py:143
  470.8 0.9 reshape.67
  471.7 0.7 copy.22
  (75 shorter events, 2.7 us)
Async XLA Ops:
  7.2 230.7 %all-reduce.2.cloned.1.call-start = ((), (), s32[]{:S(2)}) async-start(), calls=%async_computation.2 | async-start | bytes 737280 | tf_op jit(solution)/shard_map/psum | solution.py:128
  98.0 25.7 %copy-start = (f32[2,2,70,640]{3,1,2,0:T(2,128)S(1)}, f32[2,2,70,640]{3,1,2,0:T(2,128)}, u32[]{:S(2)}) copy-start(f32[2,2,70,640]{3,1,2,0:T(2,128)} %param.15) | copy-start | bytes 2150404
  122.7 0.7 copy-start.1
  123.4 258.8 %reduce-scatter.7.cloned.1.call-start = ((), (), s32[]{:S(2)}) async-start(), calls=%async_computation.4 | async-start | bytes 1114112
  124.3 114.9 %copy-start.2 = (f32[640]{0:T(1024)S(1)}, f32[640]{0:T(1024)}, u32[]{:S(2)}) copy-start(f32[640]{0:T(1024)} %param.14) | copy-start | bytes 7684
  290.8 180.0 %reduce-scatter.5.cloned.1.call-start = ((), (), s32[]{:S(2)}) async-start(), calls=%async_computation.3 | async-start | bytes 1253376 | tf_op jit(solution)/shard_map/reduce_scatter | solution.py:143
Sparse Core Ops, SparseCore 0:
  123.6 114.2 all-reduce.1
  290.9 91.2 reduce-scatter.6
  385.7 85.0 reduce-scatter.4
where the time goes:
time: 479 us
  waiting for transfers between devices  288 us (60%)
  blocking collectives  88.5 us (18%)
  other arithmetic  64.2 us (13%)
  local copies, waits for them, and re-layouts  15 us (3%)
  between operations  13.9 us (3%)
  matrix products  5.45 us (1%)
    psum x1, waiting for transfers between devices, body(): fields = lax.psum(partial_fields, 'dom')  114 us
    unnamed x4, waiting for transfers between devices  87.7 us
    reduce_scatter x1, waiting for transfers between devices, body(): lax.psum_scatter(coef_part, 'dir', scatter_dimension=1, tiled=True)  87.1 us
    all_gather x1, blocking collectives, body(): domain_rows = lax.all_gather(own_rows, 'dir', axis=1, tiled=True)  50.1 us
    convert_element_type x8, other arithmetic, phase_tile(): jnp.cos(angles).astype(jnp.bfloat16)  43.5 us
    all_gather x1, blocking collectives, body(): domain_places = lax.all_gather(positions, 'dir', axis=1, tiled=True)  38.4 us
    concatenate x1, other arithmetic, adjoint_terms(): left_side = jnp.concatenate([top_rows, low_rows], axis=0)  14.7 us
  transfers between devices with their start and end apart: 3, of which 3 were waited for; matrix products, arithmetic and copies ran while one was open for 1% of the time, Pallas kernels for 0%

commit v1 on v0

--- a/solution.py
+++ b/solution.py
@@ -125,7 +125,8 @@
     partial_fields = lax.fori_loop(
         0, blocks, forward_block, jnp.zeros((2 * C, polar.shape[0]), jnp.float32)
     )
-    fields = lax.psum(partial_fields, "dom")
+    long_array = lax.all_gather(partial_fields, "dom")
+    fields = jnp.sum(long_array, 0)
     adjoint = cotangent_rows(fields, farmap, weights)
     stacked = stacked_rows(adjoint, vectors)
 

time: 479 us -> 404 us (0.84)
  waiting for transfers between devices: 288 us -> 211 us
    psum x1 -> x0, waiting for transfers between devices: 114 us -> none  [body(): fields = lax.psum(partial_fields, 'dom')]
    all_gather x0 -> x1, waiting for transfers between devices: none -> 38.8 us  [body(): long_array = lax.all_gather(partial_fields, 'dom')]
where the time goes in v1:
time: 404 us
  waiting for transfers between devices  211 us (52%)
  blocking collectives  88.5 us (22%)
  other arithmetic  67.2 us (17%)
  local copies, waits for them, and re-layouts  14.4 us (4%)
  between operations  13.9 us (3%)
  matrix products  5.48 us (1%)
    reduce_scatter x1, waiting for transfers between devices, body(): lax.psum_scatter(coef_part, 'dir', scatter_dimension=1, tiled=True)  87.2 us
    unnamed x4, waiting for transfers between devices  84.8 us
    all_gather x1, blocking collectives, body(): domain_rows = lax.all_gather(own_rows, 'dir', axis=1, tiled=True)  50.1 us
    convert_element_type x8, other arithmetic, phase_tile(): jnp.cos(angles).astype(jnp.bfloat16)  43.5 us
    all_gather x1, waiting for transfers between devices, body(): long_array = lax.all_gather(partial_fields, 'dom')  38.8 us
    all_gather x1, blocking collectives, body(): domain_places = lax.all_gather(positions, 'dir', axis=1, tiled=True)  38.4 us
    concatenate x1, other arithmetic, adjoint_terms(): left_side = jnp.concatenate([top_rows, low_rows], axis=0)  14.7 us
  transfers between devices with their start and end apart: 3, of which 3 were waited for; matrix products, arithmetic and copies ran while one was open for 1% of the time, Pallas kernels for 0%

profile of v1, /device:TPU:8, one launch (start us, length us, event | category | flops | bytes accessed | tf_op | source)
XLA Modules:
  0.0 403.7 jit_solution(872004874940989667)
XLA Ops:
  7.2 0.7 fusion.36
  7.9 0.7 sine_multiply_fusion
  8.7 0.8 copy.18
  9.5 50.1 %all_gather.13 = bf16[140,2048]{1,0:T(8,128)(2,1)S(1)} all-gather(bf16[140,128]{1,0:T(8,128)(2,1)S(1)} %reshape.65), channel_id=1, replica_groups=mesh['dom'=16,'dir'=16] {'dir'}, dimensions={1}, use_global_device_ids=true | all-gather | bytes 609280 | tf_op jit(solution)/shard_map/all_gather | solution.py:111
  59.6 38.4 %all_gather.12 = f32[3,2048]{1,0:T(4,128)S(1)} all-gather(f32[3,128]{1,0:T(4,128)} %param.11), channel_id=1, replica_groups=mesh['dom'=16,'dir'=16] {'dir'}, dimensions={1}, use_global_device_ids=true | all-gather | bytes 26112 | tf_op jit(solution)/shard_map/all_gather | solution.py:112
  98.0 24.7 %while.29 = (s32[]{:T(128)}, f32[140,640]{1,0:T(8,128)S(1)}, bf16[140,2048]{1,0:T(8,128)(2,1)S(1)}, f32[3,2048]{1,0:T(4,128)S(1)}, f32[1,640]{1,0:T(1,128)S(1)},...) while((s32[]{:T(128)}, f32[140,640]{1,0:T(8,128)S(1)}, ...), condition=%wide.region_1.0_spmd.clone, body=%wide.region_0.0_spmd.clone.sunk | while | flops 189849616 | bytes 3953417 | solution.py:125
  98.2 5.4 %cosine_convert_fusion.5 = (bf16[512,640]{1,0:T(8,128)(2,1)S(1)}, bf16[512,640]{1,0:T(8,128)(2,1)S(1)}) fusion(f32[640]{0:T(1024)S(1)} %reduce.16, f32[512]{0:T(512)S(1)} %bitcast.85, f32[640]{0:T(1024)S(1)} %reduce.17, f32[512]{0:T(512)S(1)} %bitcast.84, f32[640]{0:T(1024)S(1)} %reduce.18, f32[512]{0:T(512)S(1)} %bitcast.83), kind=kLoop, calls=%fused_computation.35.clone.1 | loop fusion | flops 2293760 | bytes 1324544 | tf_op jit(solution)/shard_map/while/body/eval_jaxpr/convert_element_type | solution.py:20
  103.7 0.4 fusion.55
  104.3 5.4 %cosine_convert_fusion.5 = (bf16[512,640]{1,0:T(8,128)(2,1)S(1)}, bf16[512,640]{1,0:T(8,128)(2,1)S(1)}) fusion(f32[640]{0:T(1024)S(1)} %reduce.16, f32[512]{0:T(512)S(1)} %bitcast.85, f32[640]{0:T(1024)S(1)} %reduce.17, f32[512]{0:T(512)S(1)} %bitcast.84, f32[640]{0:T(1024)S(1)} %reduce.18, f32[512]{0:T(512)S(1)} %bitcast.83), kind=kLoop, calls=%fused_computation.35.clone.1 | loop fusion | flops 2293760 | bytes 1324544 | tf_op jit(solution)/shard_map/while/body/eval_jaxpr/convert_element_type | solution.py:20
  109.9 0.4 fusion.55
  110.5 5.4 %cosine_convert_fusion.5 = (bf16[512,640]{1,0:T(8,128)(2,1)S(1)}, bf16[512,640]{1,0:T(8,128)(2,1)S(1)}) fusion(f32[640]{0:T(1024)S(1)} %reduce.16, f32[512]{0:T(512)S(1)} %bitcast.85, f32[640]{0:T(1024)S(1)} %reduce.17, f32[512]{0:T(512)S(1)} %bitcast.84, f32[640]{0:T(1024)S(1)} %reduce.18, f32[512]{0:T(512)S(1)} %bitcast.83), kind=kLoop, calls=%fused_computation.35.clone.1 | loop fusion | flops 2293760 | bytes 1324544 | tf_op jit(solution)/shard_map/while/body/eval_jaxpr/convert_element_type | solution.py:20
  116.1 0.4 fusion.55
  116.7 5.4 %cosine_convert_fusion.5 = (bf16[512,640]{1,0:T(8,128)(2,1)S(1)}, bf16[512,640]{1,0:T(8,128)(2,1)S(1)}) fusion(f32[640]{0:T(1024)S(1)} %reduce.16, f32[512]{0:T(512)S(1)} %bitcast.85, f32[640]{0:T(1024)S(1)} %reduce.17, f32[512]{0:T(512)S(1)} %bitcast.84, f32[640]{0:T(1024)S(1)} %reduce.18, f32[512]{0:T(512)S(1)} %bitcast.83), kind=kLoop, calls=%fused_computation.35.clone.1 | loop fusion | flops 2293760 | bytes 1324544 | tf_op jit(solution)/shard_map/while/body/eval_jaxpr/convert_element_type | solution.py:20
  122.2 0.4 fusion.55
  122.7 0.7 copy-done.1
  123.5 0.2 reduce-scatter.7.cloned.1.call-start
  123.7 0.6 fusion.31
  124.3 38.8 %all-gather.4.cloned.1.call-done = f32[16,140,640]{2,1,0:T(8,128)} async-done(((f32[1,140,640]{2,1,0:T(8,128)}), f32[16,140,640]{2,1,0:T(8,128)}) %all-gather.4.cloned.1.call-update) | async-done | bytes 5734416 | tf_op jit(solution)/shard_map/all_gather | solution.py:128
  163.1 3.0 reduce_sum.78
  166.4 0.4 copy-done.2
  167.1 14.7 %maximum_maximum_fusion = bf16[560,1280]{1,0:T(8,128)(2,1)S(1)} fusion(bf16[280,640]{1,0:T(8,128)(2,1)S(1)} %maximum_negate_fusion, bf16[70,640]{1,0:T(8,128)(2,1)S(1)} %get-tuple-element.343, bf16[70,640]{1,0:T(8,128)(2,1)S(1)} %get-tuple-element.355, bf16[70,640]{1,0:T(8,128)(2,1)S(1)} %get-tuple-element.339, bf16[70,640]{1,0:T(8,128)(2,1)S(1)} %get-tuple-element.351, ...), kind=kLoop, calls=%fused_computation.48 | loop fusion | flops 18636800 | bytes 2508800 | tf_op jit(solution)/shard_map/while/body/eval_jaxpr/concatenate | solution.py:40
  181.8 35.2 %while.28 = (s32[]{:T(128)}, f32[4,140,512]{2,1,0:T(8,128)}, f32[4,3,512]{2,1,0:T(4,128)S(1)}, s32[4]{0:T(128)S(1)}, f32[3,2048]{1,0:T(4,128)S(1)}, /*index=5*/f...) while((s32[]{:T(128)}, f32[4,140,512]{2,1,0:T(8,128)}, ...), condition=%wide.region_11.12_spmd, body=%wide.region_7.11_spmd.sunk | while | flops 739566592 | bytes 7435559 | solution.py:140
  181.9 0.6 dynamic_slice.33
  183.2 5.4 %cosine_convert_fusion.4 = (bf16[512,640]{1,0:T(8,128)(2,1)S(1)}, bf16[512,640]{1,0:T(8,128)(2,1)S(1)}) fusion(f32[640]{0:T(1024)S(1)} %reduce.13, f32[512]{0:T(512)S(1)} %bitcast.88, f32[640]{0:T(1024)S(1)} %reduce.14, f32[512]{0:T(512)S(1)} %bitcast.87, f32[640]{0:T(1024)S(1)} %reduce.15, f32[512]{0:T(512)S(1)} %bitcast.86), kind=kLoop, calls=%fused_computation.5.clone.1 | loop fusion | flops 2293760 | bytes 1324544 | tf_op jit(solution)/shard_map/while/body/eval_jaxpr/convert_element_type | solution.py:20
  188.7 0.9 convolution_bitcast_fusion.2
  189.6 0.2 fusion.49
  189.9 0.7 fusion.50
  190.6 0.6 dynamic_slice.33
  192.0 5.4 %cosine_convert_fusion.4 = (bf16[512,640]{1,0:T(8,128)(2,1)S(1)}, bf16[512,640]{1,0:T(8,128)(2,1)S(1)}) fusion(f32[640]{0:T(1024)S(1)} %reduce.13, f32[512]{0:T(512)S(1)} %bitcast.88, f32[640]{0:T(1024)S(1)} %reduce.14, f32[512]{0:T(512)S(1)} %bitcast.87, f32[640]{0:T(1024)S(1)} %reduce.15, f32[512]{0:T(512)S(1)} %bitcast.86), kind=kLoop, calls=%fused_computation.5.clone.1 | loop fusion | flops 2293760 | bytes 1324544 | tf_op jit(solution)/shard_map/while/body/eval_jaxpr/convert_element_type | solution.py:20
  197.5 0.9 convolution_bitcast_fusion.2
  198.7 0.7 fusion.50
  199.4 0.6 dynamic_slice.33
  200.8 5.4 %cosine_convert_fusion.4 = (bf16[512,640]{1,0:T(8,128)(2,1)S(1)}, bf16[512,640]{1,0:T(8,128)(2,1)S(1)}) fusion(f32[640]{0:T(1024)S(1)} %reduce.13, f32[512]{0:T(512)S(1)} %bitcast.88, f32[640]{0:T(1024)S(1)} %reduce.14, f32[512]{0:T(512)S(1)} %bitcast.87, f32[640]{0:T(1024)S(1)} %reduce.15, f32[512]{0:T(512)S(1)} %bitcast.86), kind=kLoop, calls=%fused_computation.5.clone.1 | loop fusion | flops 2293760 | bytes 1324544 | tf_op jit(solution)/shard_map/while/body/eval_jaxpr/convert_element_type | solution.py:20
  206.3 0.9 convolution_bitcast_fusion.2
  207.2 0.2 fusion.49
  207.5 0.7 fusion.50
  208.2 0.6 dynamic_slice.33
  209.6 5.4 %cosine_convert_fusion.4 = (bf16[512,640]{1,0:T(8,128)(2,1)S(1)}, bf16[512,640]{1,0:T(8,128)(2,1)S(1)}) fusion(f32[640]{0:T(1024)S(1)} %reduce.13, f32[512]{0:T(512)S(1)} %bitcast.88, f32[640]{0:T(1024)S(1)} %reduce.14, f32[512]{0:T(512)S(1)} %bitcast.87, f32[640]{0:T(1024)S(1)} %reduce.15, f32[512]{0:T(512)S(1)} %bitcast.86), kind=kLoop, calls=%fused_computation.5.clone.1 | loop fusion | flops 2293760 | bytes 1324544 | tf_op jit(solution)/shard_map/while/body/eval_jaxpr/convert_element_type | solution.py:20
  215.0 0.9 convolution_bitcast_fusion.2
  216.3 0.8 fusion.50
  217.0 1.4 copy.23
  218.5 2.0 copy.20
  220.7 1.4 copy.27
  222.2 84.7 %reduce-scatter.7.cloned.1.call-done = f32[128,3]{1,0:T(8,128)} async-done(((f32[2048,3]{1,0:T(8,128)}), f32[128,3]{1,0:T(8,128)}) %reduce-scatter.7.cloned.1.call-update) | async-done | bytes 1552
  306.9 1.5 copy.24
  308.4 87.2 %reduce-scatter.5.cloned.1.call-done = f32[140,128]{1,0:T(8,128)} async-done(((f32[140,2048]{1,0:T(8,128)}), f32[140,128]{1,0:T(8,128)}) %reduce-scatter.5.cloned.1.call-update) | async-done | bytes 71696 | tf_op jit(solution)/shard_map/reduce_scatter | solution.py:144
  395.6 0.9 reshape.67
  396.5 0.7 copy.22
  (76 shorter events, 3.0 us)
Async XLA Ops:
  7.2 155.9 %all-gather.4.cloned.1.call-start = ((), (), s32[]{:S(2)}) async-start(), calls=%async_computation.3 | async-start | bytes 6266880 | tf_op jit(solution)/shard_map/all_gather | solution.py:128
  98.0 25.7 %copy-start = (f32[2,2,70,640]{3,1,2,0:T(2,128)S(1)}, f32[2,2,70,640]{3,1,2,0:T(2,128)}, u32[]{:S(2)}) copy-start(f32[2,2,70,640]{3,1,2,0:T(2,128)} %param.15) | copy-start | bytes 2150404
  122.7 0.8 copy-start.1
  123.5 183.4 %reduce-scatter.7.cloned.1.call-start = ((), (), s32[]{:S(2)}) async-start(), calls=%async_computation.4 | async-start | bytes 1114112
  166.1 0.7 copy-start.2
  218.4 177.1 %reduce-scatter.5.cloned.1.call-start = ((), (), s32[]{:S(2)}) async-start(), calls=%async_computation.2 | async-start | bytes 1253376 | tf_op jit(solution)/shard_map/reduce_scatter | solution.py:144
Sparse Core Ops, SparseCore 0:
  123.6 39.4 all-gather.3
  218.6 88.2 reduce-scatter.6
  310.4 85.0 reduce-scatter.4
